TPU v7x, 128 devices: a whole 4x4x4 slice. The times are simulated.
128 devices in a mesh: grp: 4 (over y), mem: 32 (over x, z, core).
Axes of the slice: x: 4, y: 4, z: 4, core: 2. Of those that a mesh axis runs over, the one named last changes fastest.
Arguments:
- features: bfloat16 [524288, 1024], P(('grp', 'mem')), may hold values from -24 to 24
- lengths: int32 [128, 2], P(('grp', 'mem')), may hold values from 512 to 2048, as said below
Outputs:
- sample_count: float32 [1], replicated
- feature_mean: float32 [1024], replicated
- covariance: float32 [1024, 1024], P(('grp', 'mem'))
Inputs may be any that keep to these rules, and one draw needn't show every extreme that they name: Every block of a device has 2048 slots; lengths count the valid leading slots.
All inputs are finite; a program needn't handle non-finite values.
Results may differ from a plain program's by a relative error of at most 0.0003.
Values sent between devices are 32-bit elements; how exact they have to be, the bound alone decides.
A program may use at most 64 MiB of HBM per device.

v0:
```python
import jax
import jax.numpy as jnp
from jax import lax
from jax.sharding import PartitionSpec as P


def body(features, lengths):
    half_rows = features.shape[0] // 2
    position = lax.broadcasted_iota(jnp.int32, (2, half_rows), 1)
    keep = (position < lengths[0][:, None]).reshape(1, 2 * half_rows).astype(jnp.bfloat16)
    masked = features * keep.reshape(2 * half_rows, 1)
    own_count = jnp.sum(lengths).astype(jnp.float32).reshape(1)
    own_sum = jnp.dot(keep, features, preferred_element_type=jnp.float32)
    total_count, total_sum = lax.psum((own_count, own_sum), ("grp", "mem"))
    global_mean = total_sum / total_count[0]
    own_mean = own_sum / own_count[0]
    offset_vec = own_mean - global_mean
    mean_part = own_mean[0]
    offset_part = offset_vec[0]
    fix = mean_part[:, None] * own_mean - offset_part[:, None] * offset_vec
    second = lax.psum_scatter(
        lax.dot_general(
            masked, masked, (((0,), (0,)), ((), ())), preferred_element_type=jnp.float32
        )
        - own_count[0] * fix,
        ("grp", "mem"),
        scatter_dimension=0,
        tiled=True,
    )
    covariance = second / (total_count[0] - 1.0)
    return (total_count, global_mean[0], covariance)


def solution(mesh):
    return jax.shard_map(
        body,
        mesh=mesh,
        in_specs=(P(("grp", "mem"), None), P(("grp", "mem"), None)),
        out_specs=(P(), P(), P(("grp", "mem"), None)),
        check_vma=False,
    )
```

profile of v0, /device:TPU:0, one launch (start us, length us, event | category | flops | bytes accessed | tf_op | source)
XLA Modules:
  0.0 757.0 jit_solution(8612201479733276785)
XLA Ops:
  7.2 0.0 reduce-scatter.2.cloned.1.call-start
  7.2 1.3 reduce_sum.9
  9.2 0.7 iota_compare_fusion
  9.9 4.6 fusion.7
  14.5 68.9 %all-reduce = (f32[1]{0:T(128)}, f32[1,1024]{1,0:T(1,128)S(1)}) all-reduce(f32[1]{0:T(128)} %bitcast, f32[1,1024]{1,0:T(1,128)S(1)} %fusion.7), channel_id=1, replica_groups=mesh['grp'=4,'mem'=32] {'grp','mem'}, use_global_device_ids=true, to_apply=%region_1.0 | all-reduce | flops 1025 | bytes 8200 | tf_op jit(solution)/shard_map/psum | solution.py:14
  83.4 1.2 fusion.6
  84.7 17.2 %multiply_subtract_fusion = f32[1024,1024]{1,0:T(8,128)} fusion(bf16[4096,1024]{1,0:T(8,128)(2,1)} %param.2, bf16[4096]{0:T(1024)(128)(2,1)S(1)} %convert_element_type.13, f32[1024]{0:T(1024)S(1)} %bitcast.18, f32[1024]{0:T(1024)S(1)} %broadcast_divide_fusion.1, f32[]{:T(128)} %convert_element_type.12), kind=kOutput, calls=%fused_computation.2 | convolution fusion | flops 8599371776 | bytes 12599300 | tf_op jit(solution)/shard_map/dot_general | solution.py:22
  101.9 0.0 reduce-scatter.2.cloned.1.call-update
  102.5 646.2 %reduce-scatter.2.cloned.1.call-done = f32[8,1024]{1,0:T(8,128)} async-done(((f32[1024,1024]{1,0:T(8,128)}), f32[8,1024]{1,0:T(8,128)}) %reduce-scatter.2.cloned.1.call-update) | async-done | bytes 32784 | tf_op jit(solution)/shard_map/reduce_scatter | solution.py:21
  748.7 1.4 broadcast_divide_fusion
  (4 shorter events, 0.1 us)
Async XLA Ops:
  7.2 741.6 %reduce-scatter.2.cloned.1.call-start = ((), (), s32[]{:S(2)}) async-start(), calls=%async_computation.1 | async-start | bytes 4227072 | tf_op jit(solution)/shard_map/reduce_scatter | solution.py:21
Sparse Core Ops, SparseCore 0:
  102.0 646.6 reduce-scatter.1
where the time goes:
time: 757 us
  waiting for transfers between devices  646 us (85%)
  blocking collectives  68.9 us (9%)
  matrix products  21.8 us (3%)
  between operations  15.4 us (2%)
    reduce_scatter x1, waiting for transfers between devices, body(): lax.psum_scatter(lax.dot_general(masked, masked, (((0,), (0,)), ((), ()))...  646 us
    psum x1, blocking collectives, body(): total_count, total_sum = lax.psum((own_count, own_sum), ('grp', 'mem'))  68.9 us
    dot_general x1, matrix products, body(): lax.dot_general(masked, masked, (((0,), (0,)), ((), ())), preferred_eleme...  17.2 us
  transfers between devices with their start and end apart: 1, of which 1 were waited for; matrix products, arithmetic and copies ran while one was open for 0% of the time, Pallas kernels for 0%

commit v1 on v0

v1 whole, which is shorter than its diff:
```python
import functools

import jax
import jax.numpy as jnp
from jax import lax
from jax.experimental import pallas as pl
from jax.experimental.pallas import tpu as pltpu
from jax.sharding import PartitionSpec as P

MESH = pl.DeviceIdType.MESH
ROWS = 4096
HALF = 2048
D = 1024
BLK = 256
LOADS = 4
KLOAD = ROWS // LOADS
UNITS = 8
ORDERS = ("yxz", "xzy", "zyx")


def kernel(
    len_ref, feat, stats_ref, cov_ref,
    xb, dacc, grid, p1, p2, p3, rc, r1, r2, r3,
    s0, sc, sx, sy, sz,
    lsem, csend, crecv, gsend, grecv, asend, arecv,
):
    y = lax.axis_index("grp")
    m = lax.axis_index("mem")
    x, z, c = m // 8, (m // 2) % 4, m % 2
    pos = {"y": y, "x": x, "z": z}

    def device(axis, d):
        at = dict(pos)
        at[axis] = (pos[axis] + d) % 4
        return (at["y"], at["x"] * 8 + at["z"] * 2 + c)

    partner = (y, x * 8 + z * 2 + (1 - c))

    def load(k):
        rows = pl.ds(pl.multiple_of(k * KLOAD, KLOAD), KLOAD)
        return pltpu.make_async_copy(feat.at[rows], xb.at[rows], lsem.at[k])

    for k in range(LOADS):
        load(k).start()

    barrier = pltpu.get_barrier_semaphore()
    pl.semaphore_signal(barrier, inc=1, device_id=partner, device_id_type=MESH)
    for axis in "xyz":
        for d in (1, 2, 3):
            pl.semaphore_signal(barrier, inc=1, device_id=device(axis, d), device_id_type=MESH)

    s0[0] = jnp.zeros((8, 128), jnp.float32)

    def first(k, sums):
        load(k).wait()
        rows = pl.ds(pl.multiple_of(k * KLOAD, KLOAD), KLOAD)
        length = len_ref[0, k // 2]
        at = lax.broadcasted_iota(jnp.int32, (KLOAD, 128), 0) + (k % 2) * KLOAD
        keep = (at < length).astype(jnp.float32).astype(jnp.bfloat16)
        out = []
        for t in range(8):
            part = xb[rows, 128 * t:128 * t + 128] * keep
            xb[rows, 128 * t:128 * t + 128] = part
            out.append(
                sums[t] + part.astype(jnp.float32).reshape(KLOAD // 8, 8, 128).sum(axis=0)
            )
        prod = lax.dot_general(
            xb[rows, 0:BLK], xb[rows, :], (((0,), (0,)), ((), ())),
            preferred_element_type=jnp.float32,
        )

        @pl.when(k == 0)
        def _():
            dacc[...] = prod

        @pl.when(k > 0)
        def _():
            dacc[...] += prod

        return tuple(out)

    sums = lax.fori_loop(
        0, LOADS, first, tuple(jnp.zeros((8, 128), jnp.float32) for _ in range(8))
    )
    for t in range(8):
        s0[0, t:t + 1, :] = jnp.sum(sums[t], axis=0, keepdims=True)
    s0[1] = jnp.full((8, 128), (len_ref[0, 0] + len_ref[0, 1]).astype(jnp.float32))

    def place(j):
        for i in range(j, 4):
            for h in range(2):
                col = BLK * (i - j) + 128 * h
                grid[2 * i + h, 16 * j:16 * j + 16] = dacc[:, col:col + 128].reshape(16, 2, 8, 128)
            if i > j:
                turned = dacc[:, BLK * (i - j):BLK * (i - j) + BLK].T
                for h in range(2):
                    grid[2 * j + h, 16 * i:16 * i + 16] = (
                        turned[:, 128 * h:128 * h + 128].reshape(16, 2, 8, 128)
                    )

    def product(j, half):
        rows = pl.ds(half * HALF, HALF)
        return lax.dot_general(
            xb[rows, BLK * j:BLK * j + BLK], xb[rows, BLK * j:], (((0,), (0,)), ((), ())),
            preferred_element_type=jnp.float32,
        )

    def pair_copy(u):
        return pltpu.make_async_remote_copy(
            src_ref=grid.at[u, :, 1 - c], dst_ref=rc.at[u],
            send_sem=csend.at[u], recv_sem=crecv.at[u],
            device_id=partner, device_id_type=MESH,
        )

    def axis_copy(u, stage, d):
        order = ORDERS[u % 3]
        axis = order[stage]
        to = (pos[axis] + d) % 4
        if stage == 0:
            src = {"y": p1.at[u, to], "x": p1.at[u, :, to], "z": p1.at[u, :, :, to]}[axis]
            dst = r1.at[u, d - 1]
        elif stage == 1:
            src = p2.at[u, :, to] if order == "xzy" else p2.at[u, to]
            dst = r2.at[u, d - 1]
        else:
            src = p3.at[u, to]
            dst = r3.at[u, d - 1]
        return pltpu.make_async_remote_copy(
            src_ref=src, dst_ref=dst,
            send_sem=gsend.at[u, stage, d - 1], recv_sem=grecv.at[u, stage, d - 1],
            device_id=device(axis, d), device_id_type=MESH,
        )

    def send_pair(u):
        pair_copy(u).start()

    def step(u, stage):
        order = ORDERS[u % 3]
        if stage == 0:
            pair_copy(u).wait_recv()
            p1[u] = grid[u, :, c].reshape(4, 4, 4, 8, 128) + rc[u].reshape(4, 4, 4, 8, 128)
        else:
            for d in (1, 2, 3):
                axis_copy(u, stage - 1, d).wait_recv()
            at = pos[order[stage - 1]]
            if stage == 1:
                own = {"y": lambda: p1[u, at], "x": lambda: p1[u, :, at], "z": lambda: p1[u, :, :, at]}[order[0]]()
                p2[u] = (own + r1[u, 0]) + (r1[u, 1] + r1[u, 2])
            elif stage == 2:
                own = p2[u, :, at] if order == "xzy" else p2[u, at]
                p3[u] = (own + r2[u, 0]) + (r2[u, 1] + r2[u, 2])
        for d in (1, 2, 3):
            axis_copy(u, stage, d).start()

    def sum_pair():
        return pltpu.make_async_remote_copy(
            src_ref=s0, dst_ref=sc, send_sem=asend.at[9], recv_sem=arecv.at[9],
            device_id=partner, device_id_type=MESH,
        )

    stages = (("x", sx), ("y", sy), ("z", sz))

    def sum_copy(i, d):
        axis, buf = stages[i]
        return pltpu.make_async_remote_copy(
            src_ref=buf.at[pos[axis]], dst_ref=buf.at[pos[axis]],
            send_sem=asend.at[3 * i + d - 1], recv_sem=arecv.at[3 * i + d - 1],
            device_id=device(axis, d), device_id_type=MESH,
        )

    def sum_step(i):
        if i == 0:
            sum_pair().wait_recv()
            value = s0[...] + sc[...]
        else:
            for d in (1, 2, 3):
                sum_copy(i - 1, d).wait_recv()
            buf = stages[i - 1][1]
            value = (buf[0] + buf[1]) + (buf[2] + buf[3])
        if i < 3:
            axis, buf = stages[i]
            buf[pos[axis]] = value
            for d in (1, 2, 3):
                sum_copy(i, d).start()
        return value

    pl.semaphore_wait(barrier, 10)
    sum_pair().start()
    place(0)
    send_pair(0)
    send_pair(1)

    dacc[:, 0:768] = product(1, 0)
    sum_step(0)
    step(0, 0)
    step(1, 0)
    dacc[:, 0:768] += product(1, 1)
    place(1)
    send_pair(2)
    send_pair(3)
    dacc[:, 0:512] = product(2, 0)
    step(2, 0)
    step(3, 0)
    dacc[:, 0:512] += product(2, 1)
    place(2)
    send_pair(4)
    send_pair(5)
    dacc[:, 0:256] = product(3, 0)
    step(4, 0)
    step(5, 0)
    dacc[:, 0:256] += product(3, 1)
    place(3)
    send_pair(6)
    send_pair(7)

    sum_step(1)
    step(0, 1)
    step(1, 1)
    step(6, 0)
    step(7, 0)
    step(2, 1)
    step(3, 1)
    sum_step(2)
    step(0, 2)
    step(1, 2)
    step(4, 1)
    step(5, 1)
    step(2, 2)
    step(3, 2)
    step(6, 1)
    step(7, 1)
    total = sum_step(3)
    step(4, 2)
    step(5, 2)
    step(6, 2)
    step(7, 2)

    count = total[1]
    mean = total[0] / count
    stats_ref[0] = mean
    stats_ref[1] = count
    index = y * 32 + m
    row = stats_ref[0, pl.ds(index // 16, 1), :]
    lane = lax.broadcasted_iota(jnp.int32, (8, 128), 1)
    sub = lax.broadcasted_iota(jnp.int32, (8, 128), 0)
    picked = jnp.where(lane == (index % 16) * 8 + sub, jnp.broadcast_to(row, (8, 128)), 0.0)
    own_mean = jnp.sum(picked, axis=1, keepdims=True)
    scale = 1.0 / (count - 1.0)
    for u in range(UNITS):
        for d in (1, 2, 3):
            axis_copy(u, 2, d).wait_recv()
        at = pos[ORDERS[u % 3][2]]
        second = (p3[u, at] + r3[u, 0]) + (r3[u, 1] + r3[u, 2])
        outer = own_mean * stats_ref[0, u:u + 1, :]
        cov_ref[:, 128 * u:128 * u + 128] = (second - count * outer) / (count - 1.0)

    sum_pair().wait_send()
    for i in range(3):
        for d in (1, 2, 3):
            sum_copy(i, d).wait_send()
    for u in range(UNITS):
        pair_copy(u).wait_send()
        for stage in range(3):
            for d in (1, 2, 3):
                axis_copy(u, stage, d).wait_send()


def body(features, lengths):
    f32 = jnp.float32
    stats, cov = pl.pallas_call(
        kernel,
        out_shape=(
            jax.ShapeDtypeStruct((2, 8, 128), f32),
            jax.ShapeDtypeStruct((8, D), f32),
        ),
        in_specs=[
            pl.BlockSpec(memory_space=pltpu.SMEM),
            pl.BlockSpec(memory_space=pl.ANY),
        ],
        out_specs=(
            pl.BlockSpec(memory_space=pltpu.VMEM),
            pl.BlockSpec(memory_space=pltpu.VMEM),
        ),
        scratch_shapes=[
            pltpu.VMEM((ROWS, D), jnp.bfloat16),
            pltpu.VMEM((BLK, D), f32),
            pltpu.VMEM((UNITS, 64, 2, 8, 128), f32),
            pltpu.VMEM((UNITS, 4, 4, 4, 8, 128), f32),
            pltpu.VMEM((UNITS, 4, 4, 8, 128), f32),
            pltpu.VMEM((UNITS, 4, 8, 128), f32),
            pltpu.VMEM((UNITS, 64, 8, 128), f32),
            pltpu.VMEM((UNITS, 3, 4, 4, 8, 128), f32),
            pltpu.VMEM((UNITS, 3, 4, 8, 128), f32),
            pltpu.VMEM((UNITS, 3, 8, 128), f32),
            pltpu.VMEM((2, 8, 128), f32),
            pltpu.VMEM((2, 8, 128), f32),
            pltpu.VMEM((4, 2, 8, 128), f32),
            pltpu.VMEM((4, 2, 8, 128), f32),
            pltpu.VMEM((4, 2, 8, 128), f32),
            pltpu.SemaphoreType.DMA((LOADS,)),
            pltpu.SemaphoreType.DMA((UNITS,)),
            pltpu.SemaphoreType.DMA((UNITS,)),
            pltpu.SemaphoreType.DMA((UNITS, 3, 3)),
            pltpu.SemaphoreType.DMA((UNITS, 3, 3)),
            pltpu.SemaphoreType.DMA((10,)),
            pltpu.SemaphoreType.DMA((10,)),
        ],
        compiler_params=pltpu.CompilerParams(
            collective_id=0, has_side_effects=True, vmem_limit_bytes=60 * 1024 * 1024
        ),
        name="gram_reduce",
    )(lengths, features)
    return stats[1, 0, 0:1], stats[0].reshape(D), cov


def solution(mesh):
    return jax.shard_map(
        body,
        mesh=mesh,
        in_specs=(P(("grp", "mem"), None), P(("grp", "mem"), None)),
        out_specs=(P(), P(), P(("grp", "mem"), None)),
        check_vma=False,
    )
```

time: 757 us -> 44.1 us (0.06)
  waiting for transfers between devices: 646 us -> 0 us
  blocking collectives: 68.9 us -> 0 us
  Pallas kernels: 0 us -> 39.4 us
  matrix products: 21.8 us -> 0 us
  between operations: 15.4 us -> 0.64 us
    reduce_scatter x1 -> x0, waiting for transfers between devices: 646 us -> none  [body(): lax.psum_scatter(lax.dot_general(masked, masked, (((0,), (0,)), ((), ()))...]
    psum x1 -> x0, blocking collectives: 68.9 us -> none  [body(): total_count, total_sum = lax.psum((own_count, own_sum), ('grp', 'mem'))]
    pallas_call x0 -> x1, Pallas kernels: none -> 39.4 us  [body(): pl.pallas_call(kernel, out_shape=(jax.ShapeDtypeStruct((2, 8, 128), f32),...]
    dot_general x2 -> x0, matrix products: 21.8 us -> none  [the longest x1 17.2 us: body(): lax.dot_general(masked, masked, (((0,), (0,)), ((), ())), preferred_eleme...]
  transfers between devices with their start and end apart: 1 -> 0, of which waited for: 1 -> 0; matrix products, arithmetic and copies ran while one was open for 0% -> 0% of each run, Pallas kernels for 0% -> 0%
where the time goes in v1:
time: 44.1 us; the launch traced here: 43.8 us
  Pallas kernels  39.4 us (89%)
  local copies, waits for them, and re-layouts  3.84 us (9%)
  between operations  0.64 us (1%)
    pallas_call x1, Pallas kernels, body(): pl.pallas_call(kernel, out_shape=(jax.ShapeDtypeStruct((2, 8, 128), f32),...  39.4 us
    unnamed x1, local copies, waits for them, and re-layouts  1.37 us
    another operation x1, local copies, waits for them, and re-layouts, body(): return (stats[1, 0, 0:1], stats[0].reshape(D), cov)  1.27 us
    slice x1, local copies, waits for them, and re-layouts, body(): return (stats[1, 0, 0:1], stats[0].reshape(D), cov)  1.19 us

profile of v1, /device:TPU:0, one launch (start us, length us, event | category | flops | bytes accessed | tf_op | source)
XLA Modules:
  0.0 43.8 jit_solution(4869146119901239776)
XLA Ops:
  0.6 39.4 %gram_reduce.1 = (f32[2,8,128]{2,1,0:T(8,128)}, f32[8,1024]{1,0:T(8,128)}) custom-call(s32[1,2]{1,0:T(1,128)} %len_ref.1, bf16[4096,1024]{1,0:T(8,128)(2,1)} %feat.1), custom_call_target="tpu_custom_call" | custom-call | tf_op jit(solution)/shard_map/gram_reduce/pallas_call | solution.py:270
  40.0 1.3 %slice_bitcast_fusion = f32[1024]{0:T(1024)} fusion(f32[2,8,128]{2,1,0:T(8,128)} %get-tuple-element.5), kind=kLoop, calls=%fused_computation | loop fusion | bytes 8192 | tf_op jit(solution)/shard_map/reshape;squeeze | solution.py:313
  41.3 1.2 %slice.6 = f32[1,1,1]{2,1,0:T(1,128)} slice(f32[2,8,128]{2,1,0:T(8,128)} %get-tuple-element.5), slice={[1:2], [0:1], [0:1]} | slice | bytes 8 | tf_op jit(solution)/shard_map/slice | solution.py:313
  42.5 1.4 %copy.6 = f32[8,1024]{1,0:T(8,128)} copy(f32[8,1024]{1,0:T(8,128)} %get-tuple-element.12) | data formatting | bytes 65536

commit v2 on v1

v2 whole, which is shorter than its diff:
```python
import functools

import jax
import jax.numpy as jnp
from jax import lax
from jax.experimental import pallas as pl
from jax.experimental.pallas import tpu as pltpu
from jax.sharding import PartitionSpec as P

MESH = pl.DeviceIdType.MESH
ROWS = 4096
D = 1024
BLK = 128
LOADS = 4
KLOAD = ROWS // LOADS
UNITS = 8
ORDERS = ("yxz", "xzy", "zyx")


def kernel(
    len_hbm, feat, stats_ref, cov_ref,
    len_ref, xb, kt, da, db, grid, p1, p2, p3, rc, r1, r2, r3,
    s0, sc, sx, sy, sz,
    nsem, lsem, csend, crecv, gsend, grecv, asend, arecv,
):
    y = lax.axis_index("grp")
    m = lax.axis_index("mem")
    x, z, c = m // 8, (m // 2) % 4, m % 2
    pos = {"y": y, "x": x, "z": z}

    def device(axis, d):
        at = dict(pos)
        at[axis] = (pos[axis] + d) % 4
        return (at["y"], at["x"] * 8 + at["z"] * 2 + c)

    partner = (y, x * 8 + z * 2 + (1 - c))

    def load(k):
        rows = pl.ds(pl.multiple_of(k * KLOAD, KLOAD), KLOAD)
        return pltpu.make_async_copy(feat.at[rows], xb.at[rows], lsem.at[k])

    lengths_copy = pltpu.make_async_copy(len_hbm, len_ref, nsem.at[0])
    lengths_copy.start()
    for k in range(LOADS):
        load(k).start()

    barrier = pltpu.get_barrier_semaphore()
    pl.semaphore_signal(barrier, inc=1, device_id=partner, device_id_type=MESH)
    for axis in "xyz":
        for d in (1, 2, 3):
            pl.semaphore_signal(barrier, inc=1, device_id=device(axis, d), device_id_type=MESH)

    da[...] = jnp.zeros(da.shape, jnp.float32)
    lengths_copy.wait()

    def first(k, carry):
        load(k).wait()
        rows = pl.ds(pl.multiple_of(k * KLOAD, KLOAD), KLOAD)
        at = lax.broadcasted_iota(jnp.int32, (16, KLOAD), 1) + (k % 2) * KLOAD
        keep = (at < len_ref[0, k // 2]).astype(jnp.float32).astype(jnp.bfloat16)
        kt[:, rows] = keep
        left = xb[rows, 0:BLK].T * jnp.concatenate([keep] * 8, axis=0)
        da[...] += jnp.dot(
            jnp.concatenate([left, keep], axis=0), xb[rows, :],
            preferred_element_type=jnp.float32,
        )
        return carry

    lax.fori_loop(0, LOADS, first, 0)
    for t in range(8):
        s0[0, t:t + 1, :] = da[BLK:BLK + 1, 128 * t:128 * t + 128]
    s0[1] = jnp.full((8, 128), (len_ref[0, 0] + len_ref[0, 1]).astype(jnp.float32))

    def put(u, i, value):
        value = value.reshape(2, 4, 2, 8, 128)
        at = 2 * (i % 2)
        for core in range(2):
            grid[u, core, i // 2, at:at + 2] = value[:, :, core]

    def place(j, dacc):
        for i in range(j, UNITS):
            part = dacc[0:BLK, BLK * (i - j):BLK * (i - j) + BLK]
            put(i, j, part)
            if i > j:
                put(j, i, part.T)

    def product(j, dacc):
        left = xb[:, BLK * j:BLK * j + BLK].T * jnp.concatenate([kt[...]] * 8, axis=0)
        dacc[0:BLK, 0:D - BLK * j] = jnp.dot(
            left, xb[:, BLK * j:], preferred_element_type=jnp.float32
        )

    def pair_copy(u):
        return pltpu.make_async_remote_copy(
            src_ref=grid.at[u, 1 - c], dst_ref=rc.at[u],
            send_sem=csend.at[u], recv_sem=crecv.at[u],
            device_id=partner, device_id_type=MESH,
        )

    def axis_copy(u, stage, d):
        axis = ORDERS[u % 3][stage]
        to = (pos[axis] + d) % 4
        src = (p1, p2, p3)[stage].at[u, to]
        dst = (r1, r2, r3)[stage].at[u, d - 1]
        return pltpu.make_async_remote_copy(
            src_ref=src, dst_ref=dst,
            send_sem=gsend.at[u, stage, d - 1], recv_sem=grecv.at[u, stage, d - 1],
            device_id=device(axis, d), device_id_type=MESH,
        )

    def send_pair(u):
        pair_copy(u).start()

    def gather(u, stage):
        order = ORDERS[u % 3]
        if stage == 0:
            pair_copy(u).wait_recv()
            if order == "yxz":
                p1[u] = grid[u, c] + rc[u]
            else:
                for i in range(4):
                    for k in range(4):
                        if order == "xzy":
                            p1[u, i, k] = grid[u, c, :, i, k] + rc[u, :, i, k]
                        else:
                            p1[u, i, k] = grid[u, c, k, :, i] + rc[u, k, :, i]
        else:
            for d in (1, 2, 3):
                axis_copy(u, stage - 1, d).wait_recv()
            src, got, dst = ((p1, r1, p2), (p2, r2, p3))[stage - 1]
            own = src[u, pos[order[stage - 1]]]
            dst[u] = (own + got[u, 0]) + (got[u, 1] + got[u, 2])

    def step(units, stage):
        for u in units:
            gather(u, stage)
        for d in (2, 1, 3):
            for u in units:
                axis_copy(u, stage, d).start()

    def sum_pair():
        return pltpu.make_async_remote_copy(
            src_ref=s0, dst_ref=sc, send_sem=asend.at[9], recv_sem=arecv.at[9],
            device_id=partner, device_id_type=MESH,
        )

    stages = (("x", sx), ("y", sy), ("z", sz))

    def sum_copy(i, d):
        axis, buf = stages[i]
        return pltpu.make_async_remote_copy(
            src_ref=buf.at[pos[axis]], dst_ref=buf.at[pos[axis]],
            send_sem=asend.at[3 * i + d - 1], recv_sem=arecv.at[3 * i + d - 1],
            device_id=device(axis, d), device_id_type=MESH,
        )

    def sum_step(i):
        if i == 0:
            sum_pair().wait_recv()
            value = s0[...] + sc[...]
        else:
            for d in (1, 2, 3):
                sum_copy(i - 1, d).wait_recv()
            buf = stages[i - 1][1]
            value = (buf[0] + buf[1]) + (buf[2] + buf[3])
        if i < 3:
            axis, buf = stages[i]
            buf[pos[axis]] = value
            for d in (1, 2, 3):
                sum_copy(i, d).start()
        return value

    pl.semaphore_wait(barrier, 10)
    sum_pair().start()

    place(0, da)
    send_pair(0)
    for j in range(1, UNITS):
        buf = (da, db)[j % 2]
        product(j, buf)
        place(j, buf)
        send_pair(j)
        if j == 1:
            sum_step(0)
            step((0,), 0)
        if j == 2:
            step((1,), 0)
    early, middle, late = (0, 1), (2, 3, 4), (5, 6, 7)
    step(middle, 0)
    step(late, 0)
    sum_step(1)
    step(early, 1)
    step(middle, 1)
    sum_step(2)
    step(early, 2)
    step(late, 1)
    step(middle, 2)
    total = sum_step(3)
    step(late, 2)

    count = total[1]
    mean = total[0] / count
    stats_ref[0] = mean
    stats_ref[1] = count
    index = y * 32 + m
    row = stats_ref[0, pl.ds(index // 16, 1), :]
    lane = lax.broadcasted_iota(jnp.int32, (8, 128), 1)
    sub = lax.broadcasted_iota(jnp.int32, (8, 128), 0)
    picked = jnp.where(lane == (index % 16) * 8 + sub, jnp.broadcast_to(row, (8, 128)), 0.0)
    own_mean = jnp.sum(picked, axis=1, keepdims=True)
    scale = 1.0 / (count - 1.0)
    for u in range(UNITS):
        for d in (1, 2, 3):
            axis_copy(u, 2, d).wait_recv()
        at = pos[ORDERS[u % 3][2]]
        second = (p3[u, at] + r3[u, 0]) + (r3[u, 1] + r3[u, 2])
        outer = own_mean * stats_ref[0, u:u + 1, :]
        cov_ref[:, 128 * u:128 * u + 128] = (second - count * outer) / (count - 1.0)

    sum_pair().wait_send()
    for i in range(3):
        for d in (1, 2, 3):
            sum_copy(i, d).wait_send()
    for u in range(UNITS):
        pair_copy(u).wait_send()
        for stage in range(3):
            for d in (1, 2, 3):
                axis_copy(u, stage, d).wait_send()


def finish(stats_ref, cov_ref, count_out, mean_out, cov_out):
    count_out[...] = stats_ref[1, 0:1, 0:1]
    mean_out[...] = stats_ref[0]
    cov_out[...] = cov_ref[...]


def body(features, lengths):
    f32 = jnp.float32
    stats, cov = pl.pallas_call(
        kernel,
        out_shape=(
            jax.ShapeDtypeStruct((2, 8, 128), f32),
            jax.ShapeDtypeStruct((8, D), f32),
        ),
        in_specs=[
            pl.BlockSpec(memory_space=pl.ANY),
            pl.BlockSpec(memory_space=pl.ANY),
        ],
        out_specs=(
            pl.BlockSpec(memory_space=pltpu.VMEM),
            pl.BlockSpec(memory_space=pltpu.VMEM),
        ),
        scratch_shapes=[
            pltpu.SMEM((1, 2), jnp.int32),
            pltpu.VMEM((ROWS, D), jnp.bfloat16),
            pltpu.VMEM((16, ROWS), jnp.bfloat16),
            pltpu.VMEM((BLK + 16, D), f32),
            pltpu.VMEM((BLK, D - BLK), f32),
            pltpu.VMEM((UNITS, 2, 4, 4, 4, 8, 128), f32),
            pltpu.VMEM((UNITS, 4, 4, 4, 8, 128), f32),
            pltpu.VMEM((UNITS, 4, 4, 8, 128), f32),
            pltpu.VMEM((UNITS, 4, 8, 128), f32),
            pltpu.VMEM((UNITS, 4, 4, 4, 8, 128), f32),
            pltpu.VMEM((UNITS, 3, 4, 4, 8, 128), f32),
            pltpu.VMEM((UNITS, 3, 4, 8, 128), f32),
            pltpu.VMEM((UNITS, 3, 8, 128), f32),
            pltpu.VMEM((2, 8, 128), f32),
            pltpu.VMEM((2, 8, 128), f32),
            pltpu.VMEM((4, 2, 8, 128), f32),
            pltpu.VMEM((4, 2, 8, 128), f32),
            pltpu.VMEM((4, 2, 8, 128), f32),
            pltpu.SemaphoreType.DMA((1,)),
            pltpu.SemaphoreType.DMA((LOADS,)),
            pltpu.SemaphoreType.DMA((UNITS,)),
            pltpu.SemaphoreType.DMA((UNITS,)),
            pltpu.SemaphoreType.DMA((UNITS, 3, 3)),
            pltpu.SemaphoreType.DMA((UNITS, 3, 3)),
            pltpu.SemaphoreType.DMA((10,)),
            pltpu.SemaphoreType.DMA((10,)),
        ],
        compiler_params=pltpu.CompilerParams(
            collective_id=0, has_side_effects=True, vmem_limit_bytes=63 * 1024 * 1024
        ),
        name="gram_reduce",
    )(lengths, features)
    count, mean, cov = pl.pallas_call(
        finish,
        out_shape=(
            jax.ShapeDtypeStruct((1, 1), f32),
            jax.ShapeDtypeStruct((8, 128), f32),
            jax.ShapeDtypeStruct((8, D), f32),
        ),
        in_specs=[pl.BlockSpec(memory_space=pltpu.VMEM)] * 2,
        out_specs=(pl.BlockSpec(memory_space=pltpu.VMEM),) * 3,
        name="finish",
    )(stats, cov)
    return count.reshape(1), mean.reshape(D), cov


def solution(mesh):
    return jax.shard_map(
        body,
        mesh=mesh,
        in_specs=(P(("grp", "mem"), None), P(("grp", "mem"), None)),
        out_specs=(P(), P(), P(("grp", "mem"), None)),
        check_vma=False,
    )
```

time: 44.1 us -> 37.9 us (0.86)
  local copies, waits for them, and re-layouts: 3.84 us -> 0 us
  Pallas kernels: 39.4 us -> 37.1 us
    pallas_call x1, Pallas kernels: 39.4 us -> 35.7 us  [body(): pl.pallas_call(kernel, out_shape=(jax.ShapeDtypeStruct((2, 8, 128), f32),...]
    pallas_call x0 -> x1, Pallas kernels: none -> 1.4 us  [body(): pl.pallas_call(finish, out_shape=(jax.ShapeDtypeStruct((1, 1), f32), jax....]
    unnamed x1 -> x0, local copies, waits for them, and re-layouts: 1.37 us -> none
    another operation x1 -> x0, local copies, waits for them, and re-layouts: 1.27 us -> none  [body(): return (stats[1, 0, 0:1], stats[0].reshape(D), cov)]
    slice x1 -> x0, local copies, waits for them, and re-layouts: 1.19 us -> none  [body(): return (stats[1, 0, 0:1], stats[0].reshape(D), cov)]
where the time goes in v2:
time: 37.9 us; the launch traced here: 37.7 us
  Pallas kernels  37.1 us (98%)
  between operations  0.64 us (2%)
    pallas_call x1, Pallas kernels, body(): pl.pallas_call(kernel, out_shape=(jax.ShapeDtypeStruct((2, 8, 128), f32),...  35.7 us
    pallas_call x1, Pallas kernels, body(): pl.pallas_call(finish, out_shape=(jax.ShapeDtypeStruct((1, 1), f32), jax....  1.4 us

profile of v2, /device:TPU:0, one launch (start us, length us, event | category | flops | bytes accessed | tf_op | source)
XLA Modules:
  0.0 37.7 jit_solution(14607220650433800481)
XLA Ops:
  0.6 35.7 %gram_reduce.1 = (f32[2,8,128]{2,1,0:T(8,128)}, f32[8,1024]{1,0:T(8,128)}) custom-call(s32[1,2]{1,0:T(1,128)} %len_hbm.1, bf16[4096,1024]{1,0:T(8,128)(2,1)} %feat.1), custom_call_target="tpu_custom_call" | custom-call | tf_op jit(solution)/shard_map/gram_reduce/pallas_call | solution.py:239
  36.3 1.4 %finish.1 = (f32[1,1]{1,0:T(1,128)}, f32[8,128]{1,0:T(8,128)}, f32[8,1024]{1,0:T(8,128)}) custom-call(f32[2,8,128]{2,1,0:T(8,128)} %get-tuple-element.8.stats_ref, f32[8,1024]{1,0:T(8,128)} %get-tuple-element.9.cov_ref), custom_call_target="tpu_custom_call" | custom-call | tf_op jit(solution)/shard_map/finish/pallas_call | solution.py:286

commit v3 on v2

--- a/solution.py
+++ b/solution.py
@@ -15,6 +15,10 @@
 KLOAD = ROWS // LOADS
 UNITS = 8
 ORDERS = ("yxz", "xzy", "zyx")
+
+
+def order_of(f, u):
+    return u % 3 if f == 3 else f
 
 
 def kernel(
@@ -97,46 +101,63 @@
             device_id=partner, device_id_type=MESH,
         )
 
-    def axis_copy(u, stage, d):
-        axis = ORDERS[u % 3][stage]
+    own_class = (x + y + z) % 4
+
+    def axis_copy(u, f, stage, d):
+        axis = ORDERS[order_of(f, u)][stage]
         to = (pos[axis] + d) % 4
-        src = (p1, p2, p3)[stage].at[u, to]
-        dst = (r1, r2, r3)[stage].at[u, d - 1]
+        src = (p1, p2)[stage].at[u, f, to]
+        dst = (r1, r2)[stage].at[u, f, d - 1]
         return pltpu.make_async_remote_copy(
             src_ref=src, dst_ref=dst,
-            send_sem=gsend.at[u, stage, d - 1], recv_sem=grecv.at[u, stage, d - 1],
+            send_sem=gsend.at[u, stage], recv_sem=grecv.at[u, stage],
             device_id=device(axis, d), device_id_type=MESH,
+        )
+
+    def last_copy(u, d):
+        f = (own_class + d) % 4
+        o = jnp.where(f == 3, u % 3, f)
+        ty = (y + jnp.where(o == 1, d, 0)) % 4
+        tx = (x + jnp.where(o == 2, d, 0)) % 4
+        tz = (z + jnp.where(o == 0, d, 0)) % 4
+        return pltpu.make_async_remote_copy(
+            src_ref=p3.at[u, f], dst_ref=r3.at[u, d - 1],
+            send_sem=gsend.at[u, 2], recv_sem=grecv.at[u, 2],
+            device_id=(ty, tx * 8 + tz * 2 + c), device_id_type=MESH,
+        )
+
+    def all_of(u, stage):
+        buf = (r1, r2, r3)[stage].at[u]
+        return pltpu.make_async_remote_copy(
+            src_ref=buf, dst_ref=buf, send_sem=gsend.at[u, stage], recv_sem=grecv.at[u, stage],
+            device_id=partner, device_id_type=MESH,
         )
 
     def send_pair(u):
         pair_copy(u).start()
 
-    def gather(u, stage):
-        order = ORDERS[u % 3]
+    def step(u, stage):
         if stage == 0:
             pair_copy(u).wait_recv()
-            if order == "yxz":
-                p1[u] = grid[u, c] + rc[u]
-            else:
+            for f in range(4):
+                order = ORDERS[order_of(f, u)]
                 for i in range(4):
                     for k in range(4):
-                        if order == "xzy":
-                            p1[u, i, k] = grid[u, c, :, i, k] + rc[u, :, i, k]
-                        else:
-                            p1[u, i, k] = grid[u, c, k, :, i] + rc[u, k, :, i]
+                        at = {order[0]: i, order[1]: k, order[2]: (f - i - k) % 4}
+                        where = (at["y"], at["x"], at["z"])
+                        p1[u, f, i, k] = grid[(u, c) + where] + rc[(u,) + where]
         else:
-            for d in (1, 2, 3):
-                axis_copy(u, stage - 1, d).wait_recv()
+            all_of(u, stage - 1).wait_recv()
             src, got, dst = ((p1, r1, p2), (p2, r2, p3))[stage - 1]
-            own = src[u, pos[order[stage - 1]]]
-            dst[u] = (own + got[u, 0]) + (got[u, 1] + got[u, 2])
-
-    def step(units, stage):
-        for u in units:
-            gather(u, stage)
+            for f in range(4):
+                own = src[u, f, pos[ORDERS[order_of(f, u)][stage - 1]]]
+                dst[u, f] = (own + got[u, f, 0]) + (got[u, f, 1] + got[u, f, 2])
         for d in (2, 1, 3):
-            for u in units:
-                axis_copy(u, stage, d).start()
+            if stage == 2:
+                last_copy(u, d).start()
+            else:
+                for f in range(4):
+                    axis_copy(u, f, stage, d).start()
 
     def sum_pair():
         return pltpu.make_async_remote_copy(
@@ -179,24 +200,28 @@
         buf = (da, db)[j % 2]
         product(j, buf)
         place(j, buf)
-        send_pair(j)
+        if j < 6:
+            send_pair(j)
         if j == 1:
             sum_step(0)
-            step((0,), 0)
+            step(0, 0)
         if j == 2:
-            step((1,), 0)
-    early, middle, late = (0, 1), (2, 3, 4), (5, 6, 7)
-    step(middle, 0)
-    step(late, 0)
-    sum_step(1)
-    step(early, 1)
-    step(middle, 1)
-    sum_step(2)
-    step(early, 2)
-    step(late, 1)
-    step(middle, 2)
+            step(1, 0)
+        if j == 3:
+            step(2, 0)
+        if j == 5:
+            step(3, 0)
+    send_pair(6)
+    send_pair(7)
+    for u, stage in (
+        (4, 0), (5, 0), (0, 1), (6, 0), (7, 0), (-1, 1), (1, 1), (2, 1), (0, 2), (3, 1), (4, 1),
+        (1, 2), (2, 2), (-1, 2), (5, 1), (6, 1), (7, 1), (3, 2), (4, 2), (5, 2), (6, 2), (7, 2),
+    ):
+        if u < 0:
+            sum_step(stage)
+        else:
+            step(u, stage)
     total = sum_step(3)
-    step(late, 2)
 
     count = total[1]
     mean = total[0] / count
@@ -210,10 +235,8 @@
     own_mean = jnp.sum(picked, axis=1, keepdims=True)
     scale = 1.0 / (count - 1.0)
     for u in range(UNITS):
-        for d in (1, 2, 3):
-            axis_copy(u, 2, d).wait_recv()
-        at = pos[ORDERS[u % 3][2]]
-        second = (p3[u, at] + r3[u, 0]) + (r3[u, 1] + r3[u, 2])
+        all_of(u, 2).wait_recv()
+        second = (p3[u, own_class] + r3[u, 0]) + (r3[u, 1] + r3[u, 2])
         outer = own_mean * stats_ref[0, u:u + 1, :]
         cov_ref[:, 128 * u:128 * u + 128] = (second - count * outer) / (count - 1.0)
 
@@ -224,8 +247,7 @@
     for u in range(UNITS):
         pair_copy(u).wait_send()
         for stage in range(3):
-            for d in (1, 2, 3):
-                axis_copy(u, stage, d).wait_send()
+            all_of(u, stage).wait_send()
 
 
 def finish(stats_ref, cov_ref, count_out, mean_out, cov_out):
@@ -261,8 +283,8 @@
             pltpu.VMEM((UNITS, 4, 4, 8, 128), f32),
             pltpu.VMEM((UNITS, 4, 8, 128), f32),
             pltpu.VMEM((UNITS, 4, 4, 4, 8, 128), f32),
-            pltpu.VMEM((UNITS, 3, 4, 4, 8, 128), f32),
-            pltpu.VMEM((UNITS, 3, 4, 8, 128), f32),
+            pltpu.VMEM((UNITS, 4, 3, 4, 8, 128), f32),
+            pltpu.VMEM((UNITS, 4, 3, 8, 128), f32),
             pltpu.VMEM((UNITS, 3, 8, 128), f32),
             pltpu.VMEM((2, 8, 128), f32),
             pltpu.VMEM((2, 8, 128), f32),
@@ -273,8 +295,8 @@
             pltpu.SemaphoreType.DMA((LOADS,)),
             pltpu.SemaphoreType.DMA((UNITS,)),
             pltpu.SemaphoreType.DMA((UNITS,)),
-            pltpu.SemaphoreType.DMA((UNITS, 3, 3)),
-            pltpu.SemaphoreType.DMA((UNITS, 3, 3)),
+            pltpu.SemaphoreType.DMA((UNITS, 3)),
+            pltpu.SemaphoreType.DMA((UNITS, 3)),
             pltpu.SemaphoreType.DMA((10,)),
             pltpu.SemaphoreType.DMA((10,)),
         ],

time: 37.9 us -> 35.3 us (0.931)
  Pallas kernels: 37.1 us -> 34.4 us
    pallas_call x1, Pallas kernels: 35.7 us -> 33 us  [body(): pl.pallas_call(kernel, out_shape=(jax.ShapeDtypeStruct((2, 8, 128), f32),...]
where the time goes in v3:
time: 35.3 us; the launch traced here: 35.1 us
  Pallas kernels  34.4 us (97%)
  between operations  0.64 us (2%)
    pallas_call x1, Pallas kernels, body(): pl.pallas_call(kernel, out_shape=(jax.ShapeDtypeStruct((2, 8, 128), f32),...  33 us
    pallas_call x1, Pallas kernels, body(): pl.pallas_call(finish, out_shape=(jax.ShapeDtypeStruct((1, 1), f32), jax....  1.4 us

profile of v3, /device:TPU:0, one launch (start us, length us, event | category | flops | bytes accessed | tf_op | source)
XLA Modules:
  0.0 35.1 jit_solution(17135897109543324598)
XLA Ops:
  0.6 33.0 %gram_reduce.1 = (f32[2,8,128]{2,1,0:T(8,128)}, f32[8,1024]{1,0:T(8,128)}) custom-call(s32[1,2]{1,0:T(1,128)} %len_hbm.1, bf16[4096,1024]{1,0:T(8,128)(2,1)} %feat.1), custom_call_target="tpu_custom_call" | custom-call | tf_op jit(solution)/shard_map/gram_reduce/pallas_call | solution.py:261
  33.7 1.4 %finish.1 = (f32[1,1]{1,0:T(1,128)}, f32[8,128]{1,0:T(8,128)}, f32[8,1024]{1,0:T(8,128)}) custom-call(f32[2,8,128]{2,1,0:T(8,128)} %get-tuple-element.8.stats_ref, f32[8,1024]{1,0:T(8,128)} %get-tuple-element.9.cov_ref), custom_call_target="tpu_custom_call" | custom-call | tf_op jit(solution)/shard_map/finish/pallas_call | solution.py:308

commit v4 on v3

--- a/solution.py
+++ b/solution.py
@@ -11,6 +11,7 @@
 ROWS = 4096
 D = 1024
 BLK = 128
+PAIR = 256
 LOADS = 4
 KLOAD = ROWS // LOADS
 UNITS = 8
@@ -63,7 +64,7 @@
         at = lax.broadcasted_iota(jnp.int32, (16, KLOAD), 1) + (k % 2) * KLOAD
         keep = (at < len_ref[0, k // 2]).astype(jnp.float32).astype(jnp.bfloat16)
         kt[:, rows] = keep
-        left = xb[rows, 0:BLK].T * jnp.concatenate([keep] * 8, axis=0)
+        left = xb[rows, 0:PAIR].T * jnp.concatenate([keep] * 16, axis=0)
         da[...] += jnp.dot(
             jnp.concatenate([left, keep], axis=0), xb[rows, :],
             preferred_element_type=jnp.float32,
@@ -72,7 +73,7 @@
 
     lax.fori_loop(0, LOADS, first, 0)
     for t in range(8):
-        s0[0, t:t + 1, :] = da[BLK:BLK + 1, 128 * t:128 * t + 128]
+        s0[0, t:t + 1, :] = da[PAIR:PAIR + 1, 128 * t:128 * t + 128]
     s0[1] = jnp.full((8, 128), (len_ref[0, 0] + len_ref[0, 1]).astype(jnp.float32))
 
     def put(u, i, value):
@@ -81,17 +82,20 @@
         for core in range(2):
             grid[u, core, i // 2, at:at + 2] = value[:, :, core]
 
-    def place(j, dacc):
-        for i in range(j, UNITS):
-            part = dacc[0:BLK, BLK * (i - j):BLK * (i - j) + BLK]
-            put(i, j, part)
-            if i > j:
-                put(j, i, part.T)
-
-    def product(j, dacc):
-        left = xb[:, BLK * j:BLK * j + BLK].T * jnp.concatenate([kt[...]] * 8, axis=0)
-        dacc[0:BLK, 0:D - BLK * j] = jnp.dot(
-            left, xb[:, BLK * j:], preferred_element_type=jnp.float32
+    def place(p, dacc):
+        for j in (2 * p, 2 * p + 1):
+            row = BLK * (j - 2 * p)
+            for i in range(j, UNITS):
+                col = BLK * (i - 2 * p)
+                part = dacc[row:row + BLK, col:col + BLK]
+                put(i, j, part)
+                if i > j:
+                    put(j, i, part.T)
+
+    def product(p, dacc):
+        left = xb[:, PAIR * p:PAIR * p + PAIR].T * jnp.concatenate([kt[...]] * 16, axis=0)
+        dacc[0:PAIR, 0:D - PAIR * p] = jnp.dot(
+            left, xb[:, PAIR * p:], preferred_element_type=jnp.float32
         )
 
     def pair_copy(u):
@@ -196,26 +200,20 @@
 
     place(0, da)
     send_pair(0)
-    for j in range(1, UNITS):
-        buf = (da, db)[j % 2]
-        product(j, buf)
-        place(j, buf)
-        if j < 6:
-            send_pair(j)
-        if j == 1:
+    send_pair(1)
+    for p in range(1, UNITS // 2):
+        buf = (da, db)[p % 2]
+        product(p, buf)
+        place(p, buf)
+        send_pair(2 * p)
+        send_pair(2 * p + 1)
+        if p == 1:
             sum_step(0)
-            step(0, 0)
-        if j == 2:
-            step(1, 0)
-        if j == 3:
-            step(2, 0)
-        if j == 5:
-            step(3, 0)
-    send_pair(6)
-    send_pair(7)
+        step(2 * p - 2, 0)
+        step(2 * p - 1, 0)
     for u, stage in (
-        (4, 0), (5, 0), (0, 1), (6, 0), (7, 0), (-1, 1), (1, 1), (2, 1), (0, 2), (3, 1), (4, 1),
-        (1, 2), (2, 2), (-1, 2), (5, 1), (6, 1), (7, 1), (3, 2), (4, 2), (5, 2), (6, 2), (7, 2),
+        (0, 1), (1, 1), (6, 0), (7, 0), (-1, 1), (2, 1), (3, 1), (0, 2), (1, 2), (4, 1), (5, 1),
+        (-1, 2), (2, 2), (3, 2), (6, 1), (7, 1), (4, 2), (5, 2), (6, 2), (7, 2),
     ):
         if u < 0:
             sum_step(stage)
@@ -265,8 +263,8 @@
             jax.ShapeDtypeStruct((8, D), f32),
         ),
         in_specs=[
-            pl.BlockSpec(memory_space=pl.ANY),
-            pl.BlockSpec(memory_space=pl.ANY),
+            pl.BlockSpec(memory_space=pltpu.HBM),
+            pl.BlockSpec(memory_space=pltpu.HBM),
         ],
         out_specs=(
             pl.BlockSpec(memory_space=pltpu.VMEM),
@@ -276,8 +274,8 @@
             pltpu.SMEM((1, 2), jnp.int32),
             pltpu.VMEM((ROWS, D), jnp.bfloat16),
             pltpu.VMEM((16, ROWS), jnp.bfloat16),
-            pltpu.VMEM((BLK + 16, D), f32),
-            pltpu.VMEM((BLK, D - BLK), f32),
+            pltpu.VMEM((PAIR + 16, D), f32),
+            pltpu.VMEM((PAIR, D - PAIR), f32),
             pltpu.VMEM((UNITS, 2, 4, 4, 4, 8, 128), f32),
             pltpu.VMEM((UNITS, 4, 4, 4, 8, 128), f32),
             pltpu.VMEM((UNITS, 4, 4, 8, 128), f32),
@@ -301,10 +299,13 @@
             pltpu.SemaphoreType.DMA((10,)),
         ],
         compiler_params=pltpu.CompilerParams(
-            collective_id=0, has_side_effects=True, vmem_limit_bytes=63 * 1024 * 1024
+            collective_id=0, has_side_effects=True, vmem_limit_bytes=40 * 1024 * 1024
         ),
         name="gram_reduce",
-    )(lengths, features)
+    )(
+        pltpu.with_memory_space_constraint(lengths, pltpu.HBM),
+        pltpu.with_memory_space_constraint(features, pltpu.HBM),
+    )
     count, mean, cov = pl.pallas_call(
         finish,
         out_shape=(
@@ -314,6 +315,7 @@
         ),
         in_specs=[pl.BlockSpec(memory_space=pltpu.VMEM)] * 2,
         out_specs=(pl.BlockSpec(memory_space=pltpu.VMEM),) * 3,
+        compiler_params=pltpu.CompilerParams(vmem_limit_bytes=1024 * 1024),
         name="finish",
     )(stats, cov)
     return count.reshape(1), mean.reshape(D), cov

time: 35.3 us -> 33.5 us (0.949)
  Pallas kernels: 34.4 us -> 32.8 us
    pallas_call x1, Pallas kernels: 33 us -> 32.1 us  [body(): pl.pallas_call(kernel, out_shape=(jax.ShapeDtypeStruct((2, 8, 128), f32),...]
    pallas_call x1, Pallas kernels: 1.4 us -> 0.63 us  [body(): pl.pallas_call(finish, out_shape=(jax.ShapeDtypeStruct((1, 1), f32), jax....]
where the time goes in v4:
time: 33.5 us; the launch traced here: 33.4 us
  Pallas kernels  32.8 us (98%)
  between operations  0.64 us (2%)
    pallas_call x1, Pallas kernels, body(): pl.pallas_call(kernel, out_shape=(jax.ShapeDtypeStruct((2, 8, 128), f32),...  32.1 us

profile of v4, /device:TPU:0, one launch (start us, length us, event | category | flops | bytes accessed | tf_op | source)
XLA Modules:
  0.0 33.4 jit_solution(12611034951398857445)
XLA Ops:
  0.6 32.1 %gram_reduce.1 = (f32[2,8,128]{2,1,0:T(8,128)S(1)}, f32[8,1024]{1,0:T(8,128)S(1)}) custom-call(s32[1,2]{1,0:T(1,128)} %len_hbm.1, bf16[4096,1024]{1,0:T(8,128)(2,1)} %feat.1), custom_call_target="tpu_custom_call" | custom-call | tf_op jit(solution)/shard_map/gram_reduce/pallas_call | solution.py:259
  32.8 0.6 %finish.1 = (f32[1,1]{1,0:T(1,128)}, f32[8,128]{1,0:T(8,128)}, f32[8,1024]{1,0:T(8,128)}) custom-call(f32[2,8,128]{2,1,0:T(8,128)S(1)} %get-tuple-element.8.stats_ref, f32[8,1024]{1,0:T(8,128)S(1)} %get-tuple-element.9.cov_ref), custom_call_target="tpu_custom_call" | custom-call | tf_op jit(solution)/shard_map/finish/pallas_call | solution.py:309

commit v5 on v4

--- a/solution.py
+++ b/solution.py
@@ -12,8 +12,7 @@
 D = 1024
 BLK = 128
 PAIR = 256
-LOADS = 4
-KLOAD = ROWS // LOADS
+LOADS = ((0, 1024), (1024, 1024), (2048, 1024), (3072, 512), (3584, 512))
 UNITS = 8
 ORDERS = ("yxz", "xzy", "zyx")
 
@@ -41,12 +40,12 @@
     partner = (y, x * 8 + z * 2 + (1 - c))
 
     def load(k):
-        rows = pl.ds(pl.multiple_of(k * KLOAD, KLOAD), KLOAD)
+        rows = pl.ds(*LOADS[k])
         return pltpu.make_async_copy(feat.at[rows], xb.at[rows], lsem.at[k])
 
     lengths_copy = pltpu.make_async_copy(len_hbm, len_ref, nsem.at[0])
     lengths_copy.start()
-    for k in range(LOADS):
+    for k in range(len(LOADS)):
         load(k).start()
 
     barrier = pltpu.get_barrier_semaphore()
@@ -55,23 +54,23 @@
         for d in (1, 2, 3):
             pl.semaphore_signal(barrier, inc=1, device_id=device(axis, d), device_id_type=MESH)
 
-    da[...] = jnp.zeros(da.shape, jnp.float32)
     lengths_copy.wait()
 
-    def first(k, carry):
+    for k, (start, size) in enumerate(LOADS):
         load(k).wait()
-        rows = pl.ds(pl.multiple_of(k * KLOAD, KLOAD), KLOAD)
-        at = lax.broadcasted_iota(jnp.int32, (16, KLOAD), 1) + (k % 2) * KLOAD
-        keep = (at < len_ref[0, k // 2]).astype(jnp.float32).astype(jnp.bfloat16)
+        rows = pl.ds(start, size)
+        at = lax.broadcasted_iota(jnp.int32, (16, size), 1) + start % 2048
+        keep = (at < len_ref[0, start // 2048]).astype(jnp.float32).astype(jnp.bfloat16)
         kt[:, rows] = keep
         left = xb[rows, 0:PAIR].T * jnp.concatenate([keep] * 16, axis=0)
-        da[...] += jnp.dot(
+        prod = jnp.dot(
             jnp.concatenate([left, keep], axis=0), xb[rows, :],
             preferred_element_type=jnp.float32,
         )
-        return carry
-
-    lax.fori_loop(0, LOADS, first, 0)
+        if k == 0:
+            da[...] = prod
+        else:
+            da[...] += prod
     for t in range(8):
         s0[0, t:t + 1, :] = da[PAIR:PAIR + 1, 128 * t:128 * t + 128]
     s0[1] = jnp.full((8, 128), (len_ref[0, 0] + len_ref[0, 1]).astype(jnp.float32))
@@ -231,7 +230,6 @@
     sub = lax.broadcasted_iota(jnp.int32, (8, 128), 0)
     picked = jnp.where(lane == (index % 16) * 8 + sub, jnp.broadcast_to(row, (8, 128)), 0.0)
     own_mean = jnp.sum(picked, axis=1, keepdims=True)
-    scale = 1.0 / (count - 1.0)
     for u in range(UNITS):
         all_of(u, 2).wait_recv()
         second = (p3[u, own_class] + r3[u, 0]) + (r3[u, 1] + r3[u, 2])
@@ -290,7 +288,7 @@
             pltpu.VMEM((4, 2, 8, 128), f32),
             pltpu.VMEM((4, 2, 8, 128), f32),
             pltpu.SemaphoreType.DMA((1,)),
-            pltpu.SemaphoreType.DMA((LOADS,)),
+            pltpu.SemaphoreType.DMA((len(LOADS),)),
             pltpu.SemaphoreType.DMA((UNITS,)),
             pltpu.SemaphoreType.DMA((UNITS,)),
             pltpu.SemaphoreType.DMA((UNITS, 3)),

time: 33.5 us -> 33.2 us (level)
  no operation moved by 1% of the time
where the time goes in v5:
time: 33.2 us; the launch traced here: 33.1 us
  Pallas kernels  32.5 us (98%)
  between operations  0.64 us (2%)
    pallas_call x1, Pallas kernels, body(): pl.pallas_call(kernel, out_shape=(jax.ShapeDtypeStruct((2, 8, 128), f32),...  31.8 us

profile of v5, /device:TPU:0, one launch (start us, length us, event | category | flops | bytes accessed | tf_op | source)
XLA Modules:
  0.0 33.1 jit_solution(15015150056036002833)
XLA Ops:
  0.6 31.8 %gram_reduce.1 = (f32[2,8,128]{2,1,0:T(8,128)S(1)}, f32[8,1024]{1,0:T(8,128)S(1)}) custom-call(s32[1,2]{1,0:T(1,128)} %len_hbm.1, bf16[4096,1024]{1,0:T(8,128)(2,1)} %feat.1), custom_call_target="tpu_custom_call" | custom-call | tf_op jit(solution)/shard_map/gram_reduce/pallas_call | solution.py:257
  32.5 0.6 %finish.1 = (f32[1,1]{1,0:T(1,128)}, f32[8,128]{1,0:T(8,128)}, f32[8,1024]{1,0:T(8,128)}) custom-call(f32[2,8,128]{2,1,0:T(8,128)S(1)} %get-tuple-element.8.stats_ref, f32[8,1024]{1,0:T(8,128)S(1)} %get-tuple-element.9.cov_ref), custom_call_target="tpu_custom_call" | custom-call | tf_op jit(solution)/shard_map/finish/pallas_call | solution.py:307

commit v6 on v5

--- a/solution.py
+++ b/solution.py
@@ -211,8 +211,26 @@
         step(2 * p - 2, 0)
         step(2 * p - 1, 0)
     for u, stage in (
-        (0, 1), (1, 1), (6, 0), (7, 0), (-1, 1), (2, 1), (3, 1), (0, 2), (1, 2), (4, 1), (5, 1),
-        (-1, 2), (2, 2), (3, 2), (6, 1), (7, 1), (4, 2), (5, 2), (6, 2), (7, 2),
+        (0, 1),
+        (6, 0),
+        (1, 1),
+        (7, 0),
+        (-1, 1),
+        (2, 1),
+        (3, 1),
+        (4, 1),
+        (5, 1),
+        (6, 1),
+        (7, 1),
+        (0, 2),
+        (1, 2),
+        (-1, 2),
+        (2, 2),
+        (3, 2),
+        (4, 2),
+        (5, 2),
+        (6, 2),
+        (7, 2),
     ):
         if u < 0:
             sum_step(stage)

time: 33.2 us -> 32.2 us (0.970)
  Pallas kernels: 32.5 us -> 31.5 us
    pallas_call x1, Pallas kernels: 31.8 us -> 30.9 us  [body(): pl.pallas_call(kernel, out_shape=(jax.ShapeDtypeStruct((2, 8, 128), f32),...]
where the time goes in v6:
time: 32.2 us; the launch traced here: 32.1 us
  Pallas kernels  31.5 us (98%)
  between operations  0.64 us (2%)
    pallas_call x1, Pallas kernels, body(): pl.pallas_call(kernel, out_shape=(jax.ShapeDtypeStruct((2, 8, 128), f32),...  30.9 us

profile of v6, /device:TPU:0, one launch (start us, length us, event | category | flops | bytes accessed | tf_op | source)
XLA Modules:
  0.0 32.1 jit_solution(4573180598608860160)
XLA Ops:
  0.6 30.9 %gram_reduce.1 = (f32[2,8,128]{2,1,0:T(8,128)S(1)}, f32[8,1024]{1,0:T(8,128)S(1)}) custom-call(s32[1,2]{1,0:T(1,128)} %len_hbm.1, bf16[4096,1024]{1,0:T(8,128)(2,1)} %feat.1), custom_call_target="tpu_custom_call" | custom-call | tf_op jit(solution)/shard_map/gram_reduce/pallas_call | solution.py:275
  31.5 0.6 %finish.1 = (f32[1,1]{1,0:T(1,128)}, f32[8,128]{1,0:T(8,128)}, f32[8,1024]{1,0:T(8,128)}) custom-call(f32[2,8,128]{2,1,0:T(8,128)S(1)} %get-tuple-element.8.stats_ref, f32[8,1024]{1,0:T(8,128)S(1)} %get-tuple-element.9.cov_ref), custom_call_target="tpu_custom_call" | custom-call | tf_op jit(solution)/shard_map/finish/pallas_call | solution.py:325

commit v7 on v6

--- a/solution.py
+++ b/solution.py
@@ -211,20 +211,20 @@
         step(2 * p - 2, 0)
         step(2 * p - 1, 0)
     for u, stage in (
+        (6, 0),
+        (7, 0),
         (0, 1),
-        (6, 0),
         (1, 1),
-        (7, 0),
-        (-1, 1),
         (2, 1),
         (3, 1),
+        (-1, 1),
         (4, 1),
         (5, 1),
         (6, 1),
         (7, 1),
+        (-1, 2),
         (0, 2),
         (1, 2),
-        (-1, 2),
         (2, 2),
         (3, 2),
         (4, 2),

time: 32.2 us -> 31.8 us (0.988)
  Pallas kernels: 31.5 us -> 31.1 us
    pallas_call x1, Pallas kernels: 30.9 us -> 30.4 us  [body(): pl.pallas_call(kernel, out_shape=(jax.ShapeDtypeStruct((2, 8, 128), f32),...]
where the time goes in v7:
time: 31.8 us; the launch traced here: 31.7 us
  Pallas kernels  31.1 us (98%)
  between operations  0.64 us (2%)
    pallas_call x1, Pallas kernels, body(): pl.pallas_call(kernel, out_shape=(jax.ShapeDtypeStruct((2, 8, 128), f32),...  30.4 us

profile of v7, /device:TPU:0, one launch (start us, length us, event | category | flops | bytes accessed | tf_op | source)
XLA Modules:
  0.0 31.7 jit_solution(15796789633463718240)
XLA Ops:
  0.6 30.4 %gram_reduce.1 = (f32[2,8,128]{2,1,0:T(8,128)S(1)}, f32[8,1024]{1,0:T(8,128)S(1)}) custom-call(s32[1,2]{1,0:T(1,128)} %len_hbm.1, bf16[4096,1024]{1,0:T(8,128)(2,1)} %feat.1), custom_call_target="tpu_custom_call" | custom-call | tf_op jit(solution)/shard_map/gram_reduce/pallas_call | solution.py:275
  31.1 0.6 %finish.1 = (f32[1,1]{1,0:T(1,128)}, f32[8,128]{1,0:T(8,128)}, f32[8,1024]{1,0:T(8,128)}) custom-call(f32[2,8,128]{2,1,0:T(8,128)S(1)} %get-tuple-element.8.stats_ref, f32[8,1024]{1,0:T(8,128)S(1)} %get-tuple-element.9.cov_ref), custom_call_target="tpu_custom_call" | custom-call | tf_op jit(solution)/shard_map/finish/pallas_call | solution.py:325
